TPU v7x, 32 devices: a whole 2x2x4 slice. The times are simulated.
32 devices in a mesh: groups: 1, expert: 16 (over z, y, core), tensor: 2 (over x).
Axes of the slice: x: 2, y: 2, z: 4, core: 2. Of those that a mesh axis runs over, the one named last changes fastest.
Arguments:
- tokens: bfloat16 [2048, 4096], P(('groups', 'expert')), may hold values from -6 to 6
- expert_ids: int32 [2048, 8], P(('groups', 'expert')), may hold values from 0 to 15, all different within a row; in each aligned block of 128 rows (0 to 127, 128 to 255, ...) at most 96 rows name the same one
- route_weights: float32 [2048, 8], P(('groups', 'expert')), may hold values from 0.1 to 1
- gate_w: bfloat16 [16, 4096, 1536], P('expert', None, 'tensor'), may hold values from -0.09375 to 0.09375
- up_w: bfloat16 [16, 4096, 1536], P('expert', None, 'tensor'), may hold values from -0.09375 to 0.09375
- down_w: bfloat16 [16, 1536, 4096], P('expert', 'tensor'), may hold values from -0.15625 to 0.15625
Outputs:
- moe_out: bfloat16 [2048, 4096], P(('groups', 'expert'), 'tensor')
Inputs may be any that keep to these rules, and one draw needn't show every extreme that they name: `expert_ids`: each row names 8 different experts. Among the rows of one device (aligned blocks of 128 rows) no expert is named more than 96 times, a bound that some block reaches.
All inputs are finite; a program needn't handle non-finite values.
Results may differ from a plain program's by a relative error of at most 0.014.
Values may be sent and summed in bfloat16 or wider, within the bound.
A program may use at most 128 MiB of HBM per device.

v0:
```python
import jax
import jax.numpy as jnp
from jax import lax
from jax.sharding import PartitionSpec as P


def shards(tokens, expert_ids, route_weights, gate_w, up_w, down_w):
    tok_rows, width = tokens.shape
    top_count = expert_ids.shape[1]
    local_experts = gate_w.shape[0]
    expert_devices = lax.axis_size("expert")
    experts_all = local_experts * expert_devices
    capacity = min(tok_rows, 3 * tok_rows * top_count // (2 * experts_all))
    flat_ids = expert_ids.reshape(-1)
    onehot = (flat_ids[:, None] == jnp.arange(experts_all, dtype=jnp.int32)[None, :]).astype(
        jnp.int32
    )
    before = jnp.cumsum(onehot, axis=0) - onehot
    slot = jnp.sum(before * onehot, axis=1)
    destination = flat_ids * capacity + slot
    token_index = jnp.arange(tok_rows * top_count, dtype=jnp.int32) // top_count
    source = jnp.zeros((experts_all * capacity,), jnp.int32).at[destination].set(token_index)
    filled = jnp.zeros((experts_all * capacity,), jnp.bool_).at[destination].set(True)
    outgoing = jnp.where(filled[:, None], tokens[source], jnp.zeros((), tokens.dtype))
    outgoing = outgoing.reshape(experts_all, capacity, tokens.shape[1])
    received = lax.all_to_all(outgoing, "expert", split_axis=0, concat_axis=0, tiled=True)
    slots_in = received.shape[1]
    rows = received.reshape(expert_devices, local_experts, slots_in, width)
    rows = rows.transpose(1, 0, 2, 3).reshape(local_experts, expert_devices * slots_in, width)
    gate = jnp.einsum("erd,edf->erf", rows, gate_w, preferred_element_type=jnp.float32)
    up_part = jnp.einsum("erd,edf->erf", rows, up_w, preferred_element_type=jnp.float32)
    hidden = (jax.nn.silu(gate) * up_part).astype(jnp.bfloat16)
    partial_value = jnp.einsum("erf,efd->erd", hidden, down_w, preferred_element_type=jnp.float32)
    summed = lax.psum_scatter(
        partial_value.astype(jnp.bfloat16), "tensor", scatter_dimension=2, tiled=True
    )
    share = summed.shape[2]
    going_back = summed.reshape(local_experts, expert_devices, slots_in, share)
    going_back = going_back.transpose(1, 0, 2, 3).reshape(experts_all, slots_in, share)
    returned = lax.all_to_all(going_back, "expert", split_axis=0, concat_axis=0, tiled=True)
    share_cols = returned.shape[2]
    flat_back = returned.reshape(experts_all * capacity, share_cols)
    picked = flat_back[destination].reshape(tok_rows, top_count, share_cols)
    mixed = jnp.einsum("tk,tkd->td", route_weights, picked.astype(jnp.float32))
    return mixed.astype(jnp.bfloat16)


def solution(mesh):
    in_specs = (
        P(("groups", "expert"), None),
        P(("groups", "expert"), None),
        P(("groups", "expert"), None),
        P("expert", None, "tensor"),
        P("expert", None, "tensor"),
        P("expert", "tensor", None),
    )
    out_specs = P(("groups", "expert"), "tensor")
    return jax.shard_map(shards, mesh=mesh, in_specs=in_specs, out_specs=out_specs, check_vma=False)
```

profile of v0, /device:TPU:13, one launch (start us, length us, event | category | flops | bytes accessed | tf_op | source)
XLA Modules:
  0.0 667.2 jit_solution(3514439401842417183)
XLA Ops:
  6.5 0.9 copy.10
  7.4 0.1 eq.29
  7.5 0.1 eq.25
  7.6 0.7 broadcast_multiply_fusion
  8.3 4.5 reduce-window.6
  12.9 0.1 copy.12
  13.1 0.1 broadcast_add_fusion
  13.2 0.1 copy.9
  13.3 0.1 mul.30
  13.5 4.3 scatter_custom_fusion.1
  17.9 4.3 scatter_custom_fusion
  22.3 9.5 %gather_fusion = bf16[1536,4096]{1,0:T(8,128)(2,1)} fusion(bf16[128,4096]{1,0:T(8,128)(2,1)S(1)} %copy-done, s32[2048]{0:T(1024)S(1)} %pad_clamp_fusion), kind=kCustom, calls=%fused_computation | custom fusion | bytes 25171968 | tf_op jit(solution)/shard_map/gather | solution.py:24
  31.8 6.4 broadcast_select_fusion
  38.2 278.6 %all_to_all.10 = bf16[16,96,4096]{2,1,0:T(8,128)(2,1)S(1)} all-to-all(bf16[16,96,4096]{2,1,0:T(8,128)(2,1)S(1)} %broadcast_select_fusion), channel_id=1, replica_groups=mesh['groups'=1,'expert'=16,'tensor'=2] {'expert'}, dimensions={0} | all-to-all | bytes 25165824 | tf_op jit(solution)/shard_map/all_to_all | solution.py:26
  316.8 11.4 %fusion.2 = f32[1536,768]{1,0:T(8,128)} fusion(bf16[1536,4096]{1,0:T(8,128)(2,1)S(1)} %bitcast.49, bf16[1,4096,768]{2,1,0:T(8,128)(2,1)S(1)} %copy-done.3), kind=kOutput, calls=%fused_computation.8 | convolution fusion | flops 9663676416 | bytes 23592960 | tf_op jit(solution)/shard_map/erd,edf->erf/dot_general | solution.py:31
  328.2 13.5 %multiply_convert_fusion = bf16[1536,768]{1,0:T(8,128)(2,1)S(1)} fusion(f32[1536,768]{1,0:T(8,128)} %fusion.2, bf16[1536,4096]{1,0:T(8,128)(2,1)S(1)} %bitcast.50, bf16[1,4096,768]{2,1,0:T(8,128)(2,1)} %param.9), kind=kOutput, calls=%fused_computation.12 | convolution fusion | flops 9670754304 | bytes 25952256 | tf_op jit(solution)/shard_map/erd,edf->erf/dot_general | solution.py:30
  341.7 12.4 %fusion = bf16[1,1536,4096]{2,1,0:T(8,128)(2,1)} fusion(bf16[1536,768]{1,0:T(8,128)(2,1)S(1)} %multiply_convert_fusion, bf16[1,768,4096]{2,1,0:T(8,128)(2,1)S(1)} %bitcast.60), kind=kOutput, calls=%fused_computation.5 | convolution fusion | flops 9669967872 | bytes 21233664 | tf_op jit(solution)/shard_map/erf,efd->erd/dot_general | solution.py:33
  354.1 145.2 %reduce-scatter.2.cloned.1.call-done = bf16[1,1536,2048]{2,1,0:T(8,128)(2,1)} async-done(((bf16[1,1536,4096]{2,1,0:T(8,128)(2,1)}), bf16[1,1536,2048]{2,1,0:T(8,128)(2,1)}) %reduce-scatter.2.cloned.1.call-update) | async-done | bytes 6291472 | tf_op jit(solution)/shard_map/reduce_scatter | solution.py:34
  499.3 6.7 all-to-all-start.1
  506.0 0.1 copy.14
  506.1 137.2 %all-to-all-done.1 = bf16[16,96,2048]{2,1,0:T(8,128)(2,1)} async-done(((bf16[16,96,2048]{2,1,0:T(8,128)(2,1)}), bf16[16,96,2048]{2,1,0:T(8,128)(2,1)}, u32[]{:S(2)}, u32[]{:S(2)}) %all-to-all-start.1) | async-done | bytes 6291488 | tf_op jit(solution)/shard_map/all_to_all | solution.py:40
  643.4 12.5 %gather_fusion.1 = bf16[1024,2048]{1,0:T(8,128)(2,1)} fusion(bf16[1536,2048]{1,0:T(8,128)(2,1)} %bitcast.11, s32[1024]{0:T(1024)S(1)} %broadcast_clamp_fusion), kind=kCustom, calls=%fused_computation.1 | custom fusion | bytes 8392704 | tf_op jit(solution)/shard_map/gather | solution.py:43
  655.9 3.4 fusion.8
  659.3 1.1 copy.19
  (28 shorter events, 0.4 us)
Async XLA Ops:
  6.5 15.8 %copy-start = (bf16[128,4096]{1,0:T(8,128)(2,1)S(1)}, bf16[128,4096]{1,0:T(8,128)(2,1)}, u32[]{:S(2)}) copy-start(bf16[128,4096]{1,0:T(8,128)(2,1)} %param.6) | copy-start | bytes 3145732
  6.5 492.8 %reduce-scatter.2.cloned.1.call-start = ((), (), s32[]{:S(2)}) async-start(), calls=%async_computation.3 | async-start | bytes 18874368 | tf_op jit(solution)/shard_map/reduce_scatter | solution.py:34
  38.2 278.6 %copy-start.3 = (bf16[1,4096,768]{2,1,0:T(8,128)(2,1)S(1)}, bf16[1,4096,768]{2,1,0:T(8,128)(2,1)}, u32[]{:S(2)}) copy-start(bf16[1,4096,768]{2,1,0:T(8,128)(2,1)} %param.10) | copy-start | bytes 18874372
  316.8 25.0 %slice-start = ((s8[6291456]{0:T(1024)(128)(4,1)}), s8[2097152]{0:T(1024)(128)(4,1)S(1)}, s32[]{:S(2)}) async-start(s8[6291456]{0:T(1024)(128)(4,1)} %bitcast.59), calls=%async_computation.4 | async-start | bytes 4194304
  328.2 13.5 %slice-start.1 = ((s8[6291456]{0:T(1024)(128)(4,1)}), s8[4194304]{0:T(1024)(128)(4,1)S(1)}, s32[]{:S(2)}) async-start(s8[6291456]{0:T(1024)(128)(4,1)} %bitcast.59), calls=%async_computation.5 | async-start | bytes 8388608
  499.3 6.7 copy-start.2
  499.3 144.1 %all-to-all-start.1 = ((bf16[16,96,2048]{2,1,0:T(8,128)(2,1)}), bf16[16,96,2048]{2,1,0:T(8,128)(2,1)}, u32[]{:S(2)}, u32[]{:S(2)}) async-start(bf16[16,96,2048]{2,1,0:T(8,128)(2,1)} %bitcast.51), calls=%async_computation.2 | async-start | bytes 12582912 | tf_op jit(solution)/shard_map/all_to_all | solution.py:40
  643.4 17.0 %copy-start.1 = (bf16[128,4096]{1,0:T(8,128)(2,1)S(1)}, bf16[128,4096]{1,0:T(8,128)(2,1)}, u32[]{:S(2)}) copy-start(bf16[128,4096]{1,0:T(8,128)(2,1)} %param.6) | copy-start | bytes 3145732
Sparse Core Ops, SparseCore 0:
  354.3 145.0 reduce-scatter.1
where the time goes:
time: 668 us; the launch traced here: 667 us
  waiting for transfers between devices  282 us (42%)
  blocking collectives  279 us (42%)
  matrix products  40.7 us (6%)
  local copies, waits for them, and re-layouts  33.6 us (5%)
  between operations  13.5 us (2%)
  other arithmetic  11.7 us (2%)
    all_to_all x1, blocking collectives, shards(): lax.all_to_all(outgoing, 'expert', split_axis=0, concat_axis=0, tiled=True)  279 us
    reduce_scatter x1, waiting for transfers between devices, shards(): lax.psum_scatter(partial_value.astype(jnp.bfloat16), 'tensor', scatter_di...  145 us
    all_to_all x1, waiting for transfers between devices, shards(): lax.all_to_all(going_back, 'expert', split_axis=0, concat_axis=0, tiled=T...  137 us
    dot_general x1, matrix products, shards(): jnp.einsum('erd,edf->erf', rows, gate_w, preferred_element_type=jnp.float32)  13.5 us
  transfers between devices with their start and end apart: 2, of which 2 were waited for; matrix products, arithmetic and copies ran while one was open for 0% of the time, Pallas kernels for 0%

commit v1 on v0

v1 whole, which is shorter than its diff:
```python
import functools

import jax
import jax.numpy as jnp
from jax import lax
from jax.experimental import pallas as pl
from jax.experimental.pallas import tpu as pltpu
from jax.sharding import PartitionSpec as P

MESH = pl.DeviceIdType.MESH
F32, BF16 = jnp.float32, jnp.bfloat16
ORDER = (
    (0, 2, 1, 4, 3, 6, 5, 7),
    (2, 0, 3, 4, 1, 6, 5, 7),
    (4, 6, 5, 2, 7, 0, 3, 1),
    (6, 4, 7, 2, 5, 0, 3, 1),
)
TARGETS = (3, 0, 2, 1)


def place():
    e = lax.axis_index("expert")
    return e, e // 4, (e // 2) % 2, e % 2, lax.axis_index("tensor")


def pick(index, values):
    out = jnp.int32(0)
    for k, v in enumerate(values):
        if v:
            out = out + jnp.where(index == k, jnp.int32(v), jnp.int32(0))
    return out


def dev(z, y, c, x):
    return {"expert": (z * 2 + y) * 2 + c, "tensor": x}


def gather_kernel(
    tok, wts, gate_hbm, up_hbm, hid, held, gate_v, up_v, wall,
    own_sem, load_sem, wsend, wrecv, zs, ys, xs, cs, cxs, rp, rx, rc, rcx,
):
    e, z, y, c, x = place()
    n_dev = wall.shape[0]
    rows = held.shape[1]
    lane = 3 * rows // 8
    main = rows - lane
    mine = pl.ds(pl.multiple_of(lane * x, 16), main)
    out_x = pl.ds(pl.multiple_of(main * x, 16), lane)
    in_x = pl.ds(pl.multiple_of(main * (1 - x), 16), lane)
    me_q = z * 2 + y

    load_own = pltpu.make_async_copy(tok, held.at[e], own_sem.at[0])
    load_own.start()
    load_gate = pltpu.make_async_copy(gate_hbm.at[0], gate_v, load_sem.at[0])
    load_up = pltpu.make_async_copy(up_hbm.at[0], up_v, load_sem.at[1])
    load_gate.start()
    load_up.start()
    load_w = pltpu.make_async_copy(wts, wall.at[e], own_sem.at[1])
    load_w.start()

    barrier = pltpu.get_barrier_semaphore()

    def greet(k, carry):
        pl.semaphore_signal(
            barrier, inc=1, device_id={"expert": (e + k) % n_dev, "tensor": x}, device_id_type=MESH
        )
        return carry

    lax.fori_loop(1, n_dev, greet, 0)
    pl.semaphore_signal(barrier, inc=1, device_id=dev(z, y, c, 1 - x), device_id_type=MESH)
    pl.semaphore_wait(barrier, n_dev)

    def cp(q, lane_c, part, send, recv, target):
        ref = held.at[q * 2 + lane_c] if part is None else held.at[q * 2 + lane_c, part]
        return pltpu.make_async_remote_copy(
            src_ref=ref, dst_ref=ref, send_sem=send, recv_sem=recv,
            device_id=target, device_id_type=MESH,
        )

    def up_copy(q):
        return cp(q, c, mine, zs.at[0, q // 2], rp.at[q], dev(jnp.minimum(z + 1, 3), y, c, x))

    def down_copy(q):
        return cp(q, c, mine, zs.at[1, q // 2], rp.at[q], dev(jnp.maximum(z - 1, 0), y, c, x))

    def y_copy(q):
        return cp(q, c, mine, ys.at[q // 2], rp.at[q], dev(z, 1 - y, c, x))

    def x_copy(q):
        return cp(q, c, out_x, xs.at[q], rx.at[q], dev(z, y, c, 1 - x))

    def x_arrive(q):
        return cp(q, c, in_x, xs.at[q], rx.at[q], dev(z, y, c, 1 - x))

    def core_copy(q, lane_c):
        return cp(q, lane_c, mine, cs.at[q], rc.at[q], dev(z, y, 1 - c, x))

    def core_x_copy(q, lane_c):
        return cp(q, lane_c, in_x, cxs.at[q], rcx.at[q], dev(z, y, 1 - c, x))

    def w_copy(k):
        return pltpu.make_async_remote_copy(
            src_ref=wall.at[e], dst_ref=wall.at[e], send_sem=wsend.at[k], recv_sem=wrecv.at[k],
            device_id={"expert": (e + k) % n_dev, "tensor": x}, device_id_type=MESH,
        )

    def w_arrive(k):
        ref = wall.at[(e + n_dev - k) % n_dev]
        return pltpu.make_async_remote_copy(
            src_ref=ref, dst_ref=ref, send_sem=wsend.at[k], recv_sem=wrecv.at[k],
            device_id={"expert": (e + k) % n_dev, "tensor": x}, device_id_type=MESH,
        )

    load_own.wait()

    @pl.when(z < 3)
    def _():
        up_copy(me_q).start()

    @pl.when(z > 0)
    def _():
        down_copy(me_q).start()

    y_copy(me_q).start()
    core_copy(me_q, c).start()
    core_x_copy(me_q, c).start()
    load_w.wait()

    def send_w(k, carry):
        w_copy(k).start()
        return carry

    lax.fori_loop(1, n_dev, send_w, 0)

    def entry(j):
        v = pick(z * 8 + j, [v for row in ORDER for v in row])
        own_y = v % 2 == 0
        return (v // 2) * 2 + jnp.where(own_y, y, 1 - y), v // 2, own_y

    def compute(q):
        a = held[pl.ds(q * 2, 2)].reshape(2 * rows, held.shape[2])
        experts = wall.shape[1]
        col = lax.broadcasted_iota(jnp.int32, (rows, experts), 1) == e
        w0 = jnp.sum(jnp.where(col, wall[q * 2].T, 0.0), axis=1, keepdims=True)
        w1 = jnp.sum(jnp.where(col, wall[q * 2 + 1].T, 0.0), axis=1, keepdims=True)
        w = jnp.concatenate([w0, w1], axis=0)
        for n in range(0, gate_v.shape[1], 256):
            g = jnp.dot(a, gate_v[:, n:n + 256], preferred_element_type=F32)
            u = jnp.dot(a, up_v[:, n:n + 256], preferred_element_type=F32)
            h = (g / (1.0 + jnp.exp(-g)) * u * w).astype(BF16)
            hid[pl.ds(q * 2, 2), :, n:n + 256] = h.reshape(2, rows, 256)

    def step(j, carry):
        @pl.when((j >= 1) & (j < 8))
        def _():
            q, zz, own_y = entry(j)
            y_copy(q).wait_recv()

            @pl.when(own_y & (zz < z) & (z < 3))
            def _():
                up_copy(q).start()

            @pl.when(own_y & (zz > z) & (z > 0))
            def _():
                down_copy(q).start()

            @pl.when(own_y)
            def _():
                y_copy(q).start()

            x_copy(q).start()
            core_copy(q, c).start()

        @pl.when((j >= 2) & (j < 9))
        def _():
            q, zz, own_y = entry(j - 1)
            x_arrive(q).wait_recv()
            core_x_copy(q, c).start()

        @pl.when(j == 0)
        def _():
            load_gate.wait()
            load_up.wait()

            def got_w(k, carry):
                w_arrive(k).wait_recv()
                return carry

            lax.fori_loop(1, n_dev, got_w, 0)

        @pl.when((j == 0) | (j >= 3))
        def _():
            q, zz, own_y = entry(jnp.where(j == 0, 0, j - 2))
            core_copy(q, 1 - c).wait_recv()
            core_x_copy(q, 1 - c).wait_recv()
            compute(q)

        return carry

    lax.fori_loop(0, 10, step, 0)

    def drain_w(k, carry):
        w_copy(k).wait_send()
        return carry

    lax.fori_loop(1, n_dev, drain_w, 0)

    def drain(j, carry):
        q, zz, own_y = entry(j)

        @pl.when(own_y & (zz <= z) & (z < 3))
        def _():
            up_copy(q).wait_send()

        @pl.when(own_y & (zz >= z) & (z > 0))
        def _():
            down_copy(q).wait_send()

        @pl.when(own_y)
        def _():
            y_copy(q).wait_send()

        @pl.when(j > 0)
        def _():
            x_copy(q).wait_send()

        core_copy(q, c).wait_send()
        core_x_copy(q, c).wait_send()
        return carry

    lax.fori_loop(0, 8, drain, 0)


def scatter_kernel(
    hid, down_hbm, out, down_v, own, oth, got_c, got_xa, got_ya, got_yb, got_xb, got_up, got_dn,
    load_sem, cs, cr, xas, xar, yas, yar, ybs, ybr, xbs, xbr, ups, upr, dns, dnr,
):
    e, z, y, c, x = place()
    rows = own.shape[1]
    top = rows // 2
    width = own.shape[2]
    half = width // 2
    load = pltpu.make_async_copy(down_hbm.at[0], down_v, load_sem.at[0])
    load.start()
    barrier = pltpu.get_barrier_semaphore()
    peer_c, peer_x, peer_y = dev(z, y, 1 - c, x), dev(z, y, c, 1 - x), dev(z, 1 - y, c, x)
    above, below = dev(jnp.minimum(z + 1, 3), y, c, x), dev(jnp.maximum(z - 1, 0), y, c, x)
    for peer in (peer_c, peer_x, peer_y):
        pl.semaphore_signal(barrier, inc=1, device_id=peer, device_id_type=MESH)

    @pl.when(z < 3)
    def _():
        pl.semaphore_signal(barrier, inc=1, device_id=above, device_id_type=MESH)

    @pl.when(z > 0)
    def _():
        pl.semaphore_signal(barrier, inc=1, device_id=below, device_id_type=MESH)

    pl.semaphore_wait(barrier, jnp.where((z == 0) | (z == 3), 4, 5))
    load.wait()

    keep = pl.ds(pl.multiple_of(x * half, 128), half)
    give = pl.ds(pl.multiple_of((1 - x) * half, 128), half)
    ra, rb = pl.ds(0, top), pl.ds(top, top)

    def rcopy(src, dst, send, recv, target):
        return pltpu.make_async_remote_copy(
            src_ref=src, dst_ref=dst, send_sem=send, recv_sem=recv,
            device_id=target, device_id_type=MESH,
        )

    def core_copy(q):
        return rcopy(oth.at[q], got_c.at[q], cs.at[q], cr.at[q], peer_c)

    def xa_copy(q):
        return rcopy(own.at[q, ra, give], got_xa.at[q], xas.at[q], xar.at[q], peer_x)

    def ya_copy(t, yy):
        return rcopy(own.at[t * 2 + yy, ra, keep], got_ya.at[t], yas.at[t], yar.at[t], peer_y)

    def yb_copy(t, yy):
        return rcopy(own.at[t * 2 + yy, rb], got_yb.at[t], ybs.at[t], ybr.at[t], peer_y)

    def xb_copy(t):
        return rcopy(own.at[t * 2 + y, rb, give], got_xb.at[t], xbs.at[t], xbr.at[t], peer_x)

    def up_copy(t):
        return rcopy(own.at[t * 2 + y, :, keep], got_up.at[t], ups.at[t], upr.at[t], above)

    def dn_copy(t):
        return rcopy(own.at[t * 2 + y, :, keep], got_dn.at[t], dns.at[t], dnr.at[t], below)

    def entry(j):
        t = pick(j // 2, TARGETS)
        return t, jnp.where(j % 2 == 0, 1 - y, y)

    def add(q, r, cols, other):
        own[q, r, cols] = (own[q, r, cols].astype(F32) + other.astype(F32)).astype(BF16)

    def stage_a(j):
        t, yy = entry(j)
        q = t * 2 + yy
        theirs = hid[q * 2 + 1 - c]
        ours = hid[q * 2 + c]
        both = jnp.concatenate([theirs, ours], axis=0)
        for n in range(0, width, 512):
            p = jnp.dot(both, down_v[:, n:n + 512], preferred_element_type=F32).astype(BF16)
            oth[q, :, n:n + 512] = p[:rows]
            own[q, :, n:n + 512] = p[rows:]
        core_copy(q).start()

    def stage_b(j):
        t, yy = entry(j)
        q = t * 2 + yy
        core_copy(q).wait_recv()
        add(q, slice(None), slice(None), got_c[q])
        xa_copy(q).start()

        @pl.when(yy != y)
        def _():
            yb_copy(t, yy).start()

    def stage_c(j):
        t, yy = entry(j)
        q = t * 2 + yy
        xa_copy(q).wait_recv()
        add(q, ra, keep, got_xa[q])

        @pl.when(yy != y)
        def _():
            ya_copy(t, yy).start()

        @pl.when(yy == y)
        def _():
            yb_copy(t, yy).wait_recv()
            add(q, rb, slice(None), got_yb[t])
            xb_copy(t).start()

    def stage_d(i):
        t = pick(i, TARGETS)
        q = t * 2 + y
        ya_copy(t, y).wait_recv()
        add(q, ra, keep, got_ya[t])
        xb_copy(t).wait_recv()
        add(q, rb, keep, got_xb[t])

        @pl.when((t > z) & (z > 0))
        def _():
            up_copy(t).wait_recv()
            add(q, slice(None), keep, got_up[t])

        @pl.when(t > z)
        def _():
            up_copy(t).start()

        @pl.when((t < z) & (z < 3))
        def _():
            dn_copy(t).wait_recv()
            add(q, slice(None), keep, got_dn[t])

        @pl.when(t < z)
        def _():
            dn_copy(t).start()

    def step(j, carry):
        @pl.when(j < 8)
        def _():
            stage_a(j)

        @pl.when((j >= 1) & (j < 9))
        def _():
            stage_b(j - 1)

        @pl.when((j >= 3) & (j < 11))
        def _():
            stage_c(j - 3)

        @pl.when((j >= 6) & (j % 2 == 0))
        def _():
            stage_d((j - 6) // 2)

        return carry

    lax.fori_loop(0, 13, step, 0)

    @pl.when(z > 0)
    def _():
        up_copy(z).wait_recv()
        add(z * 2 + y, slice(None), keep, got_up[z])

    @pl.when(z < 3)
    def _():
        dn_copy(z).wait_recv()
        add(z * 2 + y, slice(None), keep, got_dn[z])

    out[...] = own[z * 2 + y, :, keep]

    def drain(q, carry):
        core_copy(q).wait_send()
        xa_copy(q).wait_send()
        return carry

    lax.fori_loop(0, 8, drain, 0)

    def drain_t(t, carry):
        ya_copy(t, 1 - y).wait_send()
        yb_copy(t, 1 - y).wait_send()
        xb_copy(t).wait_send()

        @pl.when(t > z)
        def _():
            up_copy(t).wait_send()

        @pl.when(t < z)
        def _():
            dn_copy(t).wait_send()

        return carry

    lax.fori_loop(0, 4, drain_t, 0)


def dense_weights(expert_ids, route_weights, experts):
    hit = expert_ids[None] == jnp.arange(experts, dtype=jnp.int32)[:, None, None]
    return jnp.sum(jnp.where(hit, route_weights[None], 0.0), axis=2)


def on_box(tokens, expert_ids, route_weights, gate_w, up_w, down_w):
    rows, width = tokens.shape
    n_dev = lax.axis_size("expert")
    hidden_units = gate_w.shape[2]
    wts = dense_weights(expert_ids, route_weights, n_dev)
    any_ = pl.BlockSpec(memory_space=pl.ANY)
    vmem = pl.BlockSpec(memory_space=pltpu.VMEM)
    sem = lambda *s: pltpu.SemaphoreType.DMA(s)
    half = width // 2
    hid = pl.pallas_call(
        gather_kernel,
        out_shape=jax.ShapeDtypeStruct((n_dev, rows, hidden_units), BF16),
        in_specs=[any_] * 4,
        out_specs=vmem,
        scratch_shapes=[
            pltpu.VMEM((n_dev, rows, width), BF16),
            pltpu.VMEM((width, hidden_units), BF16),
            pltpu.VMEM((width, hidden_units), BF16),
            pltpu.VMEM((n_dev, n_dev, rows), F32),
            sem(2), sem(2), sem(n_dev), sem(n_dev), sem(2, 4), sem(4),
            sem(8), sem(8), sem(8), sem(8), sem(8), sem(8), sem(8),
        ],
        compiler_params=pltpu.CompilerParams(
            collective_id=0, has_side_effects=True, vmem_limit_bytes=60 * 2**20
        ),
        name="gather_up",
    )(tokens, wts, gate_w, up_w)
    big = lambda n, r, w: pltpu.VMEM((n, r, w), BF16)
    return pl.pallas_call(
        scatter_kernel,
        out_shape=jax.ShapeDtypeStruct((rows, half), BF16),
        in_specs=[vmem, any_],
        out_specs=vmem,
        scratch_shapes=[
            pltpu.VMEM((hidden_units, width), BF16),
            big(8, rows, width), big(8, rows, width), big(8, rows, width),
            big(8, rows // 2, half), big(4, rows // 2, half),
            big(4, rows // 2, width), big(4, rows // 2, half),
            big(4, rows, half), big(4, rows, half),
            sem(1), sem(8), sem(8), sem(8), sem(8), sem(4), sem(4), sem(4), sem(4),
            sem(4), sem(4), sem(4), sem(4), sem(4), sem(4),
        ],
        compiler_params=pltpu.CompilerParams(
            collective_id=1, has_side_effects=True, vmem_limit_bytes=62 * 2**20
        ),
        name="down_scatter",
    )(hid, down_w)


def anywhere(tokens, expert_ids, route_weights, gate_w, up_w, down_w):
    rows, width = tokens.shape
    local_experts = gate_w.shape[0]
    experts = local_experts * lax.axis_size("expert")
    first = lax.axis_index("expert") * local_experts
    wts = dense_weights(expert_ids, route_weights, experts)
    every = lax.all_gather(tokens, "expert", axis=0, tiled=True)
    wall = lax.all_gather(wts, "expert", axis=1, tiled=True)
    total = None
    for i in range(local_experts):
        w = lax.dynamic_index_in_dim(wall, first + i, 0, keepdims=False)[:, None]
        g = jnp.dot(every, gate_w[i], preferred_element_type=F32)
        u = jnp.dot(every, up_w[i], preferred_element_type=F32)
        h = (jax.nn.silu(g) * u * w).astype(BF16)
        p = jnp.dot(h, down_w[i], preferred_element_type=F32)
        total = p if total is None else total + p
    mixed = lax.psum_scatter(total.astype(BF16), "expert", scatter_dimension=0, tiled=True)
    return lax.psum_scatter(mixed, "tensor", scatter_dimension=1, tiled=True)


def solution(mesh):
    shape = dict(mesh.shape)
    box = shape == {"groups": 1, "expert": 16, "tensor": 2}
    in_specs = (
        P(("groups", "expert"), None),
        P(("groups", "expert"), None),
        P(("groups", "expert"), None),
        P("expert", None, "tensor"),
        P("expert", None, "tensor"),
        P("expert", "tensor", None),
    )
    out_specs = P(("groups", "expert"), "tensor")
    return jax.shard_map(
        on_box if box else anywhere, mesh=mesh, in_specs=in_specs, out_specs=out_specs, check_vma=False
    )
```

time: 668 us -> 226 us (0.34)
  waiting for transfers between devices: 282 us -> 0 us
  blocking collectives: 279 us -> 0 us
  Pallas kernels: 0 us -> 221 us
  matrix products: 40.7 us -> 0 us
  local copies, waits for them, and re-layouts: 33.6 us -> 1.88 us
  between operations: 13.5 us -> 0.02 us
  other arithmetic: 11.7 us -> 1.32 us
    all_to_all x1 -> x0, blocking collectives: 279 us -> none  [shards(): lax.all_to_all(outgoing, 'expert', split_axis=0, concat_axis=0, tiled=True)]
    pallas_call x0 -> x2, Pallas kernels: none -> 221 us  [the longest x1 123 us: on_box(): pl.pallas_call(scatter_kernel, out_shape=jax.ShapeDtypeStruct((rows, half...]
    reduce_scatter x1 -> x0, waiting for transfers between devices: 145 us -> none  [shards(): lax.psum_scatter(partial_value.astype(jnp.bfloat16), 'tensor', scatter_di...]
    all_to_all x1 -> x0, waiting for transfers between devices: 137 us -> none  [shards(): lax.all_to_all(going_back, 'expert', split_axis=0, concat_axis=0, tiled=T...]
    dot_general x4 -> x0, matrix products: 40.7 us -> none  [the longest x1 13.5 us: shards(): jnp.einsum('erd,edf->erf', rows, gate_w, preferred_element_type=jnp.float32)]
    gather x2 -> x0, local copies, waits for them, and re-layouts: 22 us -> none  [the longest x1 12.5 us: shards(): picked = flat_back[destination].reshape(tok_rows, top_count, share_cols)]
    scatter x2 -> x0, local copies, waits for them, and re-layouts: 8.66 us -> none  [the longest x1 4.34 us: shards(): jnp.zeros((experts_all * capacity,), jnp.bool_).at[destination].set(True)]
  transfers between devices with their start and end apart: 2 -> 0, of which waited for: 2 -> 0; matrix products, arithmetic and copies ran while one was open for 0% -> 0% of each run, Pallas kernels for 0% -> 0%
where the time goes in v1:
time: 226 us; the launch traced here: 225 us
  Pallas kernels  221 us (98%)
    pallas_call x1, Pallas kernels, on_box(): pl.pallas_call(scatter_kernel, out_shape=jax.ShapeDtypeStruct((rows, half...  123 us
    pallas_call x1, Pallas kernels, on_box(): pl.pallas_call(gather_kernel, out_shape=jax.ShapeDtypeStruct((n_dev, rows...  98.6 us

profile of v1, /device:TPU:13, one launch (start us, length us, event | category | flops | bytes accessed | tf_op | source)
XLA Modules:
  0.0 224.6 jit_solution(9269293492585259069)
XLA Ops:
  0.0 1.3 select_reduce_fusion.wts
  1.3 98.6 %gather_up.1.hid = bf16[16,128,768]{2,1,0:T(8,128)(2,1)} custom-call(bf16[128,4096]{1,0:T(8,128)(2,1)} %tok.1, f32[16,128]{1,0:T(8,128)} %select_reduce_fusion.wts, bf16[1,4096,768]{2,1,0:T(8,128)(2,1)} %gate_hbm.1, bf16[1,4096,768]{2,1,0:T(8,128)(2,1)} %up_hbm.1), custom_call_target="tpu_custom_call" | custom-call | tf_op jit(solution)/shard_map/gather_up/pallas_call | solution.py:437
  99.9 122.8 %down_scatter.1 = bf16[128,2048]{1,0:T(8,128)(2,1)} custom-call(bf16[16,128,768]{2,1,0:T(8,128)(2,1)} %gather_up.1.hid, bf16[1,768,4096]{2,1,0:T(8,128)(2,1)} %down_hbm.1), custom_call_target="tpu_custom_call" | custom-call | tf_op jit(solution)/shard_map/down_scatter/pallas_call | solution.py:456
  222.7 1.9 copy.10

commit v2 on v1

--- a/solution.py
+++ b/solution.py
@@ -16,6 +16,8 @@
     (6, 4, 7, 2, 5, 0, 3, 1),
 )
 TARGETS = (3, 0, 2, 1)
+X_LAG, UP_LAG = 3, 4
+JOIN_LAG, LAST_LAG, CHAIN_LAG = 4, 7, 12
 
 
 def place():
@@ -171,9 +173,9 @@
             x_copy(q).start()
             core_copy(q, c).start()
 
-        @pl.when((j >= 2) & (j < 9))
-        def _():
-            q, zz, own_y = entry(j - 1)
+        @pl.when((j >= 1 + X_LAG) & (j < 8 + X_LAG))
+        def _():
+            q, zz, own_y = entry(j - X_LAG)
             x_arrive(q).wait_recv()
             core_x_copy(q, c).start()
 
@@ -188,16 +190,16 @@
 
             lax.fori_loop(1, n_dev, got_w, 0)
 
-        @pl.when((j == 0) | (j >= 3))
-        def _():
-            q, zz, own_y = entry(jnp.where(j == 0, 0, j - 2))
+        @pl.when((j == 0) | (j >= 1 + UP_LAG))
+        def _():
+            q, zz, own_y = entry(jnp.where(j == 0, 0, j - UP_LAG))
             core_copy(q, 1 - c).wait_recv()
             core_x_copy(q, 1 - c).wait_recv()
             compute(q)
 
         return carry
 
-    lax.fori_loop(0, 10, step, 0)
+    lax.fori_loop(0, 8 + UP_LAG, step, 0)
 
     def drain_w(k, carry):
         w_copy(k).wait_send()
@@ -344,22 +346,28 @@
         xb_copy(t).wait_recv()
         add(q, rb, keep, got_xb[t])
 
+        @pl.when((t > z) & (z == 0))
+        def _():
+            up_copy(t).start()
+
+        @pl.when((t < z) & (z == 3))
+        def _():
+            dn_copy(t).start()
+
+    def stage_e(i):
+        t = pick(i, TARGETS)
+        q = t * 2 + y
+
         @pl.when((t > z) & (z > 0))
         def _():
             up_copy(t).wait_recv()
             add(q, slice(None), keep, got_up[t])
-
-        @pl.when(t > z)
-        def _():
             up_copy(t).start()
 
         @pl.when((t < z) & (z < 3))
         def _():
             dn_copy(t).wait_recv()
             add(q, slice(None), keep, got_dn[t])
-
-        @pl.when(t < z)
-        def _():
             dn_copy(t).start()
 
     def step(j, carry):
@@ -371,17 +379,21 @@
         def _():
             stage_b(j - 1)
 
-        @pl.when((j >= 3) & (j < 11))
-        def _():
-            stage_c(j - 3)
-
-        @pl.when((j >= 6) & (j % 2 == 0))
-        def _():
-            stage_d((j - 6) // 2)
-
-        return carry
-
-    lax.fori_loop(0, 13, step, 0)
+        @pl.when((j >= JOIN_LAG) & (j < 8 + JOIN_LAG))
+        def _():
+            stage_c(j - JOIN_LAG)
+
+        @pl.when((j >= LAST_LAG) & (j < 8 + LAST_LAG) & ((j - LAST_LAG) % 2 == 0))
+        def _():
+            stage_d((j - LAST_LAG) // 2)
+
+        @pl.when((j >= CHAIN_LAG) & ((j - CHAIN_LAG) % 2 == 0))
+        def _():
+            stage_e((j - CHAIN_LAG) // 2)
+
+        return carry
+
+    lax.fori_loop(0, 7 + CHAIN_LAG, step, 0)
 
     @pl.when(z > 0)
     def _():

time: 226 us -> 219 us (0.969); the launches traced: 225 us -> 215 us
  Pallas kernels: 221 us -> 212 us
    pallas_call x1, Pallas kernels: 123 us -> 113 us  [on_box(): pl.pallas_call(scatter_kernel, out_shape=jax.ShapeDtypeStruct((rows, half...]
where the time goes in v2:
time: 219 us; the launch traced here: 215 us
  Pallas kernels  212 us (97%)
    pallas_call x1, Pallas kernels, on_box(): pl.pallas_call(scatter_kernel, out_shape=jax.ShapeDtypeStruct((rows, half...  113 us
    pallas_call x1, Pallas kernels, on_box(): pl.pallas_call(gather_kernel, out_shape=jax.ShapeDtypeStruct((n_dev, rows...  98.6 us

profile of v2, /device:TPU:13, one launch (start us, length us, event | category | flops | bytes accessed | tf_op | source)
XLA Modules:
  0.0 215.0 jit_solution(9308168471985957454)
XLA Ops:
  0.0 1.3 select_reduce_fusion.wts
  1.3 98.6 %gather_up.1.hid = bf16[16,128,768]{2,1,0:T(8,128)(2,1)} custom-call(bf16[128,4096]{1,0:T(8,128)(2,1)} %tok.1, f32[16,128]{1,0:T(8,128)} %select_reduce_fusion.wts, bf16[1,4096,768]{2,1,0:T(8,128)(2,1)} %gate_hbm.1, bf16[1,4096,768]{2,1,0:T(8,128)(2,1)} %up_hbm.1), custom_call_target="tpu_custom_call" | custom-call | tf_op jit(solution)/shard_map/gather_up/pallas_call | solution.py:449
  99.9 113.2 %down_scatter.1 = bf16[128,2048]{1,0:T(8,128)(2,1)} custom-call(bf16[16,128,768]{2,1,0:T(8,128)(2,1)} %gather_up.1.hid, bf16[1,768,4096]{2,1,0:T(8,128)(2,1)} %down_hbm.1), custom_call_target="tpu_custom_call" | custom-call | tf_op jit(solution)/shard_map/down_scatter/pallas_call | solution.py:468
  213.1 1.9 copy.10
